TPU v7x, 256 devices: a whole 4x4x8 slice. The times are simulated.
256 devices in a mesh: pool: 8 (over z), tp: 32 (over x, y, core).
Axes of the slice: x: 4, y: 4, z: 8, core: 2. Of those that a mesh axis runs over, the one named last changes fastest.
Arguments:
- tokens: bfloat16 [4096, 8192], P(('pool', 'tp')), may hold values from -4 to 4
- lengths: int32 [8, 4], P('pool'), may hold values from 1 to 256, 512 in all within a row
- hit_pages: int32 [8, 4, 4], P('pool'), may hold values from 0 to 4095, as said below
- new_owner: int32 [8, 16], P('pool'), may hold values from 0 to 7, as said below
- w_query: bfloat16 [8192, 8192], P('pool', 'tp'), may hold values from -0.125 to 0.125
- w_keyval: bfloat16 [4096, 4096], P('pool', 'tp'), may hold values from -0.0625 to 0.0625
- w_out: bfloat16 [8192, 8192], P('tp', 'pool'), may hold values from -0.0625 to 0.0625
- pool_pages: bfloat16 [4096, 32, 2048], P('pool', 'tp'), may hold values from -65 to 65
Outputs:
- mixed: float32 [4096, 8192], P(('pool', 'tp'))
- new_store: bfloat16 [128, 32, 2048], P('pool', 'tp')
Inputs may be any that keep to these rules, and one draw needn't show every extreme that they name: Page p of the pool lies on pool index p // 512. In every group g at most 6 of the 16 entries of hit_pages[g] lie on one pool index, and some pool index holds exactly 6 of them in every group. A page may appear more than once. `new_owner`: in every group at most 2 of its 16 pages go to one pool index, and some pool index receives exactly 2 from every group. Row g holds the lengths of the 4 requests packed in group g, in order, and sums to 512.
All inputs are finite; a program needn't handle non-finite values.
Results may differ from a plain program's by a relative error of at most 0.009.
Values may be sent and summed in bfloat16 or wider, within the bound.
No kernel may reach another device: no remote copies, remote signals or barrier semaphores. Data moves between devices by JAX's collectives and lax.ppermute only.
A program may use at most 64 MiB of HBM per device.

v0:
```python
import math
import jax
import jax.numpy as jnp
from jax import lax
from jax.sharding import PartitionSpec as P

KVH = 8
HD = 128
PAGE = 32
REQS = 4
HITS = 4
CAPF = 6
CAPN = 2
EPSILON = 1e-06
ROPE_BASE = 1000000.0


def in_one_piece(arrays, axis, dim, along):
    ends, at = ([], 0)
    for a in arrays[:-1]:
        at += a.shape[along]
        ends.append(at)
    both = jnp.concatenate(arrays, axis=along)
    return tuple(jnp.split(lax.all_gather(both, axis, axis=dim, tiled=True), ends, axis=along))


def partner(value, axis, stride):
    mask = 2**stride
    pairs = [(source, source ^ mask) for source in range(lax.axis_size(axis))]
    return lax.ppermute(value, axis, pairs)


def rotate(values, positions):
    half = values.shape[-1] // 2
    steps_range = jnp.arange(half, dtype=jnp.float32)
    frequency = ROPE_BASE ** (-2.0 * steps_range / values.shape[-1])
    angles = positions.astype(jnp.float32)[:, None, None] * frequency[None, None, :]
    cosine = jnp.cos(angles)
    sine = jnp.sin(angles)
    first_half = values[..., :half]
    second_half = values[..., half:]
    return jnp.concatenate(
        [first_half * cosine - second_half * sine, second_half * cosine + first_half * sine],
        axis=-1,
    )


def slot_table(owners_row, capacity, seats):
    count_items = owners_row.shape[0]
    item_index = jnp.arange(count_items, dtype=jnp.int32)
    earlier_same = (owners_row[:, None] == owners_row[None, :]) & (
        item_index[None, :] < item_index[:, None]
    )
    slots = jnp.sum(earlier_same.astype(jnp.int32), axis=1)
    targets = owners_row * capacity + slots
    seat_index = jnp.arange(seats, dtype=jnp.int32)
    return targets[:, None] == seat_index[None, :]


def join_stack(held_new, held_cached, upper_half, other_new, other_cached):
    held_new = jnp.where(
        upper_half,
        jnp.concatenate([other_new, held_new], axis=0),
        jnp.concatenate([held_new, other_new], axis=0),
    )
    held_cached = jnp.where(
        upper_half,
        jnp.concatenate([other_cached, held_cached], axis=0),
        jnp.concatenate([held_cached, other_cached], axis=0),
    )
    return (held_new, held_cached)


def unstack_columns(held):
    return held.transpose(1, 0, 2).reshape(held.shape[1], held.shape[0] * held.shape[2])


def body(tokens, lengths, hit_pages, new_owner, w_query, w_keyval, w_out, pool_pages):
    rows_dev = tokens.shape[0]
    tp_count = lax.axis_size("tp")
    pool_count = lax.axis_size("pool")
    tp_rank = lax.axis_index("tp")
    group_rows = rows_dev * tp_count
    query_width = w_query.shape[1]
    part_width = w_keyval.shape[1] // 2
    heads_here = query_width // HD
    sharing = tp_count // KVH
    pages_here = pool_pages.shape[0]
    keyval_local = w_keyval.reshape(w_keyval.shape[0] * 2, part_width)
    pages_flat = pool_pages.reshape(pages_here, pool_pages.shape[1] * pool_pages.shape[2])
    tokens_wide = tokens.astype(jnp.float32)
    normed = (
        tokens_wide
        * lax.rsqrt(jnp.mean(tokens_wide * tokens_wide, axis=1, keepdims=True) + EPSILON)
    ).astype(jnp.bfloat16)
    full_query, full_keyval = in_one_piece((w_query, keyval_local), "pool", 0, 1)
    row_piece = lax.all_gather(normed, "tp", axis=0, tiled=True)
    projected = jnp.concatenate(
        [
            jnp.dot(row_piece, full_query, preferred_element_type=jnp.float32),
            jnp.dot(row_piece, full_keyval, preferred_element_type=jnp.float32),
        ],
        axis=1,
    )
    lengths_row = lengths[0]
    ends_at = jnp.cumsum(lengths_row)
    starts_at = ends_at - lengths_row
    token_index = jnp.arange(group_rows, dtype=jnp.int32)
    request_ids = jnp.sum((token_index[:, None] >= ends_at[None, :]).astype(jnp.int32), axis=1)
    chosen = request_ids[:, None] == jnp.arange(REQS, dtype=jnp.int32)[None, :]
    start_of = jnp.sum(jnp.where(chosen, starts_at[None, :], 0), axis=1)
    positions = token_index - start_of + HITS * PAGE
    queries = rotate(
        projected[:, :query_width].reshape(group_rows, heads_here, HD), positions
    ).astype(jnp.bfloat16)
    keyval_part = projected[:, query_width:].astype(jnp.bfloat16)
    page_ids = hit_pages.reshape(-1)
    count_hits = page_ids.shape[0]
    placed_hits = slot_table(page_ids // pages_here, CAPF, pool_count * CAPF)
    wanted = jnp.sum(jnp.where(placed_hits, (page_ids % pages_here)[:, None], 0), axis=0)
    wanted = wanted.reshape(pool_count, CAPF)
    asked = lax.all_to_all(wanted, "pool", split_axis=0, concat_axis=0, tiled=True)
    found = jnp.take(pages_flat, asked.reshape(-1), axis=0)
    found = found.reshape(asked.shape[0], asked.shape[1], pages_flat.shape[1])
    returned = lax.all_to_all(found, "pool", split_axis=0, concat_axis=0, tiled=True)
    returned = returned.reshape(pool_count * CAPF, PAGE * part_width)
    cached_part = jnp.dot(
        placed_hits.astype(jnp.bfloat16), returned, preferred_element_type=jnp.float32
    ).astype(jnp.bfloat16)
    cached_part = cached_part.reshape(count_hits * PAGE, part_width)
    bit_count = sharing.bit_length() - 1
    held_new = keyval_part[None]
    held_cached = cached_part[None]
    for bit_number in range(bit_count):
        other_new, other_cached = partner((held_new, held_cached), "tp", bit_number)
        upper_half = tp_rank // 2**bit_number % 2 == 1
        held_new, held_cached = join_stack(
            held_new, held_cached, upper_half, other_new, other_cached
        )
    new_head = unstack_columns(held_new)
    cached_head = unstack_columns(held_cached)
    new_keys = (
        rotate(new_head[:, :HD].astype(jnp.float32).reshape(group_rows, 1, HD), positions)
        .astype(jnp.bfloat16)
        .reshape(group_rows, HD)
    )
    stored_head = jnp.concatenate([new_keys, new_head[:, HD:]], axis=1)
    own_columns = lax.dynamic_slice_in_dim(
        stored_head, tp_rank % sharing * part_width, part_width, 1
    )
    page_count = group_rows // PAGE
    page_rows = own_columns.reshape(page_count, PAGE * part_width)
    placed_new = slot_table(new_owner[0], CAPN, pool_count * CAPN).astype(jnp.bfloat16)
    outgoing = jnp.dot(placed_new.T, page_rows, preferred_element_type=jnp.float32).astype(
        jnp.bfloat16
    )
    outgoing = outgoing.reshape(pool_count, CAPN, PAGE * part_width)
    new_store = lax.all_to_all(outgoing, "pool", split_axis=0, concat_axis=0, tiled=True).reshape(
        pool_count * CAPN, 1, PAGE * part_width
    )
    keys_all = jnp.concatenate([cached_head[:, :HD], new_keys], axis=0)
    values_all = jnp.concatenate([cached_head[:, HD:], new_head[:, HD:]], axis=0)
    cached_rows = count_hits * PAGE
    key_request = jnp.concatenate(
        [jnp.arange(cached_rows, dtype=jnp.int32) // (HITS * PAGE), request_ids]
    )
    key_order = jnp.concatenate([jnp.full((cached_rows,), -1, jnp.int32), token_index])
    block_rows = min(group_rows, 512)

    def attend(first_row):
        scores = jnp.einsum(
            "bhd,kd->hbk", queries, keys_all, preferred_element_type=jnp.float32
        ) / math.sqrt(HD)
        visible = (request_ids[:, None] == key_request[None, :]) & (
            key_order[None, :] <= token_index[:, None]
        )
        scores = jnp.where(visible[None], scores, -jnp.inf)
        highest = jnp.max(scores, axis=-1, keepdims=True)
        expanded = jnp.exp(scores - highest)
        weights = (expanded / jnp.sum(expanded, axis=-1, keepdims=True)).astype(jnp.bfloat16)
        blended = jnp.einsum(
            "hbk,kd->bhd", weights, values_all, preferred_element_type=jnp.float32
        ).astype(jnp.bfloat16)
        return blended.reshape(block_rows, query_width)

    attended = lax.map(
        attend, jnp.arange(group_rows // block_rows, dtype=jnp.int32) * block_rows
    ).reshape(group_rows, query_width)
    full_out = lax.all_gather(w_out, "pool", axis=1, tiled=True)
    summed = lax.psum_scatter(
        jnp.dot(attended, full_out, preferred_element_type=jnp.float32).astype(jnp.bfloat16),
        "tp",
        scatter_dimension=0,
        tiled=True,
    ).astype(jnp.float32)
    mixed = tokens_wide + summed
    return (mixed, new_store)


def solution(mesh):
    return jax.shard_map(
        body,
        mesh=mesh,
        in_specs=(
            P(("pool", "tp"), None),
            P("pool", None),
            P("pool", None, None),
            P("pool", None),
            P("pool", "tp"),
            P("pool", "tp"),
            P("tp", "pool"),
            P("pool", "tp", None),
        ),
        out_specs=(P(("pool", "tp"), None), P("pool", "tp", None)),
        check_vma=False,
    )
```

profile of v0, /device:TPU:2, one launch (start us, length us, event | category | flops | bytes accessed | tf_op | source)
XLA Modules:
  0.0 323.8 jit_solution(13723968068413563517)
XLA Ops:
  7.3 1.2 reshape.404
  8.4 2.0 pad_maximum_fusion
  10.6 1.1 fusion.18
  11.7 1.8 fusion.19
  13.6 0.7 all-gather.8.cloned.1.call-update
  14.4 0.2 convert_reduce_fusion.2
  14.6 0.7 all_to_all.12
  15.3 8.5 %all-to-all-start = ((s32[8,1,6]{2,1,0:T(1,128)}), s32[8,1,6]{2,1,0:T(1,128)S(1)}, u32[]{:S(2)}, u32[]{:S(2)}) async-start(s32[8,1,6]{2,1,0:T(1,128)} %bitcast), calls=%async_computation | async-start | bytes 8192 | tf_op jit(solution)/shard_map/all_to_all | solution.py:122
  23.8 0.2 reduce-window.4
  24.2 7.4 %all-to-all-done = s32[8,1,6]{2,1,0:T(1,128)S(1)} async-done(((s32[8,1,6]{2,1,0:T(1,128)}), s32[8,1,6]{2,1,0:T(1,128)S(1)}, u32[]{:S(2)}, u32[]{:S(2)}) %all-to-all-start) | async-done | bytes 224 | tf_op jit(solution)/shard_map/all_to_all | solution.py:122
  31.5 0.5 broadcast.349
  32.0 0.7 reduce.3
  32.8 0.7 gather_fusion
  33.6 0.8 broadcast_select_fusion
  34.4 3.4 %all-to-all-start.1 = ((bf16[8,6,2048]{2,1,0:T(8,128)(2,1)}), bf16[8,6,2048]{2,1,0:T(8,128)(2,1)S(1)}, u32[]{:S(2)}, u32[]{:S(2)}) async-start(bf16[8,6,2048]{2,1,0:T(8,128)(2,1)} %broadcast_select_fusion), calls=%async_computation.1 | async-start | bytes 524288 | tf_op jit(solution)/shard_map/all_to_all | solution.py:125
  37.9 1.5 fusion.8
  39.4 13.0 %all-to-all-done.1 = bf16[8,6,2048]{2,1,0:T(8,128)(2,1)S(1)} async-done(((bf16[8,6,2048]{2,1,0:T(8,128)(2,1)}), bf16[8,6,2048]{2,1,0:T(8,128)(2,1)S(1)}, u32[]{:S(2)}, u32[]{:S(2)}) %all-to-all-start.1) | async-done | bytes 196640 | tf_op jit(solution)/shard_map/all_to_all | solution.py:125
  52.5 0.2 convolution_convert_fusion.2
  52.7 0.2 broadcast_in_dim_reshape.3
  53.1 1.2 collective-permute-done
  54.3 1.7 collective-permute-start.1
  56.0 1.8 multiply_cosine_fusion
  57.8 2.2 collective-permute-done.1
  60.0 0.7 maximum_select_fusion
  60.7 33.0 %all-gather.6.cloned.1.call-done = bf16[8192,320]{1,0:T(8,128)(2,1)} async-done(((bf16[1024,320]{1,0:T(8,128)(2,1)}), bf16[8192,320]{1,0:T(8,128)(2,1)}) %all-gather.6.cloned.1.call-update) | async-done | bytes 5242896 | tf_op jit(solution)/shard_map/all_gather | solution.py:24
  93.7 59.0 %all-gather.4.cloned.1.call-done = bf16[512,8192]{1,0:T(8,128)(2,1)} async-done(((bf16[16,8192]{1,0:T(8,128)(2,1)}), bf16[512,8192]{1,0:T(8,128)(2,1)}) %all-gather.4.cloned.1.call-update) | async-done | bytes 8388624 | tf_op jit(solution)/shard_map/all_gather | solution.py:97
  152.7 6.8 %fusion.15 = bf16[1,512,64]{1,2,0:T(8,128)(2,1)S(1)} fusion(bf16[512,8192]{1,0:T(8,128)(2,1)} %all-gather.4.cloned.1.call-done, bf16[8192,320]{1,0:T(8,128)(2,1)} %all-gather.6.cloned.1.call-done), kind=kOutput, calls=%fused_computation.21 | convolution fusion | flops 536903680 | bytes 10551296 | tf_op jit(solution)/shard_map/dot_general | solution.py:101
  159.4 0.3 collective-permute-start.2
  159.8 4.6 %fusion.1 = f32[512,256]{0,1:T(8,128)S(1)} fusion(bf16[512,8192]{1,0:T(8,128)(2,1)S(1)} %copy-done.1, bf16[8192,320]{1,0:T(8,128)(2,1)} %all-gather.6.cloned.1.call-done), kind=kOutput, calls=%fused_computation.3 | convolution fusion | flops 2147483648 | bytes 13107200 | tf_op jit(solution)/shard_map/dot_general | solution.py:100
  164.4 0.2 copy.58
  164.7 0.2 copy.59
  164.9 0.4 collective-permute-start.3
  165.3 1.9 subtract_convert_fusion
  167.2 3.6 %collective-permute-done.3 = bf16[2,512,64]{1,2,0:T(8,128)(2,1)S(1)} collective-permute-done((bf16[2,512,64]{1,2,0:T(8,128)(2,1)S(1)}, bf16[2,512,64]{1,2,0:T(8,128)(2,1)S(1)}, u32[]{:S(2)}, u32[]{:S(2)}) %collective-permute-start.3) | collective-permute-done | bytes 131104 | tf_op jit(solution)/shard_map/ppermute | solution.py:30
  170.9 1.0 fusion.54
  172.1 1.2 fusion.33
  173.4 4.8 %fusion.56 = (f32[2,512]{1,0:T(2,128)S(1)}, f32[2,512,1024]{1,2,0:T(8,128)}) fusion(pred[512,1024]{0,1:T(8,128)(4,1)} %fusion.8, bf16[512,64]{1,0:T(8,128)(2,1)S(1)} %get-tuple-element.25, bf16[512,64]{1,0:T(8,128)(2,1)S(1)} %get-tuple-element.24, bf16[512,128]{1,0:T(8,128)(2,1)S(1)} %copy.56, bf16[512,2,64]{2,0,1:T(8,128)(2,1)} %get-tuple-element.21, ...), kind=kOutput, calls=%fused_computation.109 | convolution fusion | flops 273941504 | bytes 5246976 | tf_op jit(solution)/shard_map/while/body/eval_jaxpr/sub | solution.py:179
  178.2 2.7 fusion.11
  180.8 28.1 %all-gather.8.cloned.1.call-done = bf16[256,8192]{1,0:T(8,128)(2,1)} async-done(((bf16[256,1024]{1,0:T(8,128)(2,1)}), bf16[256,8192]{1,0:T(8,128)(2,1)}) %all-gather.8.cloned.1.call-update) | async-done | bytes 4194320 | tf_op jit(solution)/shard_map/all_gather | solution.py:189
  208.9 7.8 %convolution_convert_fusion = bf16[512,8192]{1,0:T(8,128)(2,1)} fusion(bf16[512,256]{0,1:T(8,128)(2,1)S(1)} %bitcast.70, bf16[256,8192]{1,0:T(8,128)(2,1)} %all-gather.8.cloned.1.call-done), kind=kOutput, calls=%fused_computation.2 | convolution fusion | flops 2151677952 | bytes 12845056 | tf_op jit(solution)/shard_map/dot_general | solution.py:191
  216.7 0.6 copy-done.6
  217.3 0.2 convert_reduce_fusion
  218.0 0.2 reshape.412
  218.2 0.3 convolution_convert_fusion.1
  218.5 12.5 %all_to_all.19 = bf16[8,2,2048]{2,1,0:T(2,128)(2,1)S(1)} all-to-all(bf16[8,2,2048]{2,1,0:T(2,128)(2,1)S(1)} %reshape.413), channel_id=1, replica_groups=mesh['pool'=8,'tp'=32] {'pool'}, dimensions={0} | all-to-all | bytes 131072 | tf_op jit(solution)/shard_map/all_to_all | solution.py:158
  231.0 0.7 reshape.414
  231.7 83.8 %reduce-scatter.2.cloned.1.call-done = bf16[16,8192]{1,0:T(8,128)(2,1)} async-done(((bf16[512,8192]{1,0:T(8,128)(2,1)}), bf16[16,8192]{1,0:T(8,128)(2,1)}) %reduce-scatter.2.cloned.1.call-update) | async-done | bytes 262160 | tf_op jit(solution)/shard_map/reduce_scatter | solution.py:190
  315.5 1.8 convert_add_fusion
  (54 shorter events, 1.9 us)
Async XLA Ops:
  7.2 25.6 %copy-start = (bf16[512,1,2048]{2,0,1:T(8,128)(2,1)S(1)}, bf16[512,1,2048]{2,0,1:T(8,128)(2,1)}, u32[]{:S(2)}) copy-start(bf16[512,1,2048]{2,0,1:T(8,128)(2,1)} %param.15) | copy-start | bytes 6291460
  7.2 30.7 %copy-start.3 = (s32[1024]{0:T(1024)S(1)}, s32[1024]{0:T(1024)}, u32[]{:S(2)}) copy-start(s32[1024]{0:T(1024)} %constant.140.clone.1) | copy-start | bytes 12292
  7.2 7.1 %copy-start.4 = (s32[1,4,4]{2,1,0:T(4,128)S(1)}, s32[1,4,4]{2,1,0:T(4,128)}, u32[]{:S(2)}) copy-start(s32[1,4,4]{2,1,0:T(4,128)} %param.10) | copy-start | bytes 196
  7.2 16.6 %copy-start.5 = (s32[1,4]{1,0:T(1,128)S(1)}, s32[1,4]{1,0:T(1,128)}, u32[]{:S(2)}) copy-start(s32[1,4]{1,0:T(1,128)} %param.9) | copy-start | bytes 52
  7.2 86.5 %all-gather.6.cloned.1.call-start = ((), (), s32[]{:S(2)}) async-start(), calls=%async_computation.5 | async-start | bytes 7077888 | tf_op jit(solution)/shard_map/all_gather | solution.py:24
  10.5 142.2 %all-gather.4.cloned.1.call-start = ((), (), s32[]{:S(2)}) async-start(), calls=%async_computation.4 | async-start | bytes 8650752 | tf_op jit(solution)/shard_map/all_gather | solution.py:97
  13.5 195.4 %all-gather.8.cloned.1.call-start = ((), (), s32[]{:S(2)}) async-start(), calls=%async_computation.6 | async-start | bytes 4718592 | tf_op jit(solution)/shard_map/all_gather | solution.py:189
  15.3 16.2 %all-to-all-start = ((s32[8,1,6]{2,1,0:T(1,128)}), s32[8,1,6]{2,1,0:T(1,128)S(1)}, u32[]{:S(2)}, u32[]{:S(2)}) async-start(s32[8,1,6]{2,1,0:T(1,128)} %bitcast), calls=%async_computation | async-start | bytes 8192 | tf_op jit(solution)/shard_map/all_to_all | solution.py:122
  34.4 18.0 %all-to-all-start.1 = ((bf16[8,6,2048]{2,1,0:T(8,128)(2,1)}), bf16[8,6,2048]{2,1,0:T(8,128)(2,1)S(1)}, u32[]{:S(2)}, u32[]{:S(2)}) async-start(bf16[8,6,2048]{2,1,0:T(8,128)(2,1)} %broadcast_select_fusion), calls=%async_computation.1 | async-start | bytes 524288 | tf_op jit(solution)/shard_map/all_to_all | solution.py:125
  37.8 277.7 %reduce-scatter.2.cloned.1.call-start = ((), (), s32[]{:S(2)}) async-start(), calls=%async_computation.7 | async-start | bytes 8650752 | tf_op jit(solution)/shard_map/reduce_scatter | solution.py:190
  53.0 1.3 collective-permute-start
  54.3 5.6 %collective-permute-start.1 = (bf16[2,512,64]{1,2,0:T(8,128)(2,1)S(1)}, bf16[2,512,64]{1,2,0:T(8,128)(2,1)S(1)}, u32[]{:S(2)}, u32[]{:S(2)}) collective-permute-start(bf16[2,512,64]{1,2,0:T(8,128)(2,1)S(1)} %maximum_select_fusion.2), channel_id=1, source_target_pairs={{0,2},{1,3},{2,0},{3,1},{4,6},{5,7},{6,4},{7,5},{8,10},{9,11},{10,... | collective-permute-start | bytes 393224 | tf_op jit(solution)/shard_map/ppermute | solution.py:30
  152.7 7.1 %copy-start.1 = (bf16[512,8192]{1,0:T(8,128)(2,1)S(1)}, bf16[512,8192]{1,0:T(8,128)(2,1)}, u32[]{:S(2)}) copy-start(bf16[512,8192]{1,0:T(8,128)(2,1)} %all-gather.4.cloned.1.call-done) | copy-start | bytes 25165828
  159.4 5.4 %collective-permute-start.2 = (bf16[1,512,64]{1,2,0:T(8,128)(2,1)S(1)}, bf16[1,512,64]{1,2,0:T(8,128)(2,1)S(1)}, u32[]{:S(2)}, u32[]{:S(2)}) collective-permute-start(bf16[1,512,64]{1,2,0:T(8,128)(2,1)S(1)} %fusion.15), channel_id=1, source_target_pairs={{0,1},{1,0},{2,3},{3,2},{4,5},{5,4},{6,7},{7,6},{8,9},{9,8},{10,11... | collective-permute-start | bytes 196616 | tf_op jit(solution)/shard_map/ppermute | solution.py:30
  164.9 5.9 %collective-permute-start.3 = (bf16[2,512,64]{1,2,0:T(8,128)(2,1)S(1)}, bf16[2,512,64]{1,2,0:T(8,128)(2,1)S(1)}, u32[]{:S(2)}, u32[]{:S(2)}) collective-permute-start(bf16[2,512,64]{1,2,0:T(8,128)(2,1)S(1)} %maximum_select_fusion.3), channel_id=1, source_target_pairs={{0,2},{1,3},{2,0},{3,1},{4,6},{5,7},{6,4},{7,5},{8,10},{9,11},{10,... | collective-permute-start | bytes 393224 | tf_op jit(solution)/shard_map/ppermute | solution.py:30
  216.7 0.7 copy-start.6
  216.7 98.8 %copy-start.2 = (bf16[16,8192]{1,0:T(8,128)(2,1)S(1)}, bf16[16,8192]{1,0:T(8,128)(2,1)}, u32[]{:S(2)}) copy-start(bf16[16,8192]{1,0:T(8,128)(2,1)} %param.8) | copy-start | bytes 786436
Sparse Core Ops, SparseCore 0:
  10.6 83.0 all-gather.5
  96.2 56.3 all-gather.3
  154.5 54.4 all-gather.7
  216.8 98.6 reduce-scatter.1
where the time goes:
time: 324 us
  waiting for transfers between devices  232 us (72%)
  matrix products  27.1 us (8%)
  other arithmetic  16.5 us (5%)
  starting transfers between devices  14.5 us (4%)
  between operations  14.1 us (4%)
  blocking collectives  12.5 us (4%)
  local copies, waits for them, and re-layouts  7.18 us (2%)
    reduce_scatter x1, waiting for transfers between devices, body(): lax.psum_scatter(jnp.dot(attended, full_out, preferred_element_type=jnp.f...  83.8 us
    all_gather x1, waiting for transfers between devices, body(): row_piece = lax.all_gather(normed, 'tp', axis=0, tiled=True)  59 us
    all_gather x1, waiting for transfers between devices, in_one_piece(): lax.all_gather(both, axis, axis=dim, tiled=True)  33 us
    all_gather x1, waiting for transfers between devices, body(): full_out = lax.all_gather(w_out, 'pool', axis=1, tiled=True)  28.1 us
    all_to_all x1, waiting for transfers between devices, body(): lax.all_to_all(found, 'pool', split_axis=0, concat_axis=0, tiled=True)  13 us
    all_to_all x1, blocking collectives, body(): lax.all_to_all(outgoing, 'pool', split_axis=0, concat_axis=0, tiled=True)  12.5 us
    all_to_all x1, starting transfers between devices, body(): lax.all_to_all(wanted, 'pool', split_axis=0, concat_axis=0, tiled=True)  8.47 us
    dot_general x1, matrix products, body(): jnp.dot(attended, full_out, preferred_element_type=jnp.float32)  7.77 us
  transfers between devices with their start and end apart: 10, of which 9 were waited for; matrix products, arithmetic and copies ran while one was open for 11% of the time, Pallas kernels for 0%

commit v1 on v0

--- a/solution.py
+++ b/solution.py
@@ -94,7 +94,9 @@
         * lax.rsqrt(jnp.mean(tokens_wide * tokens_wide, axis=1, keepdims=True) + EPSILON)
     ).astype(jnp.bfloat16)
     full_query, full_keyval = in_one_piece((w_query, keyval_local), "pool", 0, 1)
-    row_piece = lax.all_gather(normed, "tp", axis=0, tiled=True)
+    row_piece = jnp.concatenate(
+        lax.all_to_all(jnp.stack([normed] * lax.axis_size("tp")), "tp", 0, 0), axis=0
+    )
     projected = jnp.concatenate(
         [
             jnp.dot(row_piece, full_query, preferred_element_type=jnp.float32),

time: 324 us -> 333 us (1.028)
  starting transfers between devices: 14.5 us -> 34 us
  waiting for transfers between devices: 232 us -> 213 us
  local copies, waits for them, and re-layouts: 7.18 us -> 19.9 us
  other arithmetic: 16.5 us -> 11 us
    ppermute x4, waiting for transfers between devices: 7.03 us -> 95.4 us  [partner(): return lax.ppermute(value, axis, pairs)]
    all_gather x1 -> x0, waiting for transfers between devices: 59 us -> none  [body(): row_piece = lax.all_gather(normed, 'tp', axis=0, tiled=True)]
    all_gather x1, waiting for transfers between devices: 33 us -> 0.01 us  [in_one_piece(): lax.all_gather(both, axis, axis=dim, tiled=True)]
    all_gather x1, waiting for transfers between devices: 28.1 us -> 0.02 us  [body(): full_out = lax.all_gather(w_out, 'pool', axis=1, tiled=True)]
    ppermute x4, starting transfers between devices: 2.5 us -> 14.2 us  [partner(): return lax.ppermute(value, axis, pairs)]
    dot_general x0 -> x2, local copies, waits for them, and re-layouts: none -> 8.57 us  [body(): jnp.dot(row_piece, full_query, preferred_element_type=jnp.float32)]
    all_to_all x0 -> x1, starting transfers between devices: none -> 7.81 us  [body(): lax.all_to_all(jnp.stack([normed] * lax.axis_size('tp')), 'tp', 0, 0)]
    all_to_all x0 -> x1, waiting for transfers between devices: none -> 7.14 us  [body(): lax.all_to_all(jnp.stack([normed] * lax.axis_size('tp')), 'tp', 0, 0)]
  transfers between devices with their start and end apart: 10 -> 10, of which waited for: 9 -> 7; matrix products, arithmetic and copies ran while one was open for 11% -> 14% of each run, Pallas kernels for 0% -> 0%
where the time goes in v1:
time: 333 us; the launch traced here: 332 us
  waiting for transfers between devices  213 us (64%)
  starting transfers between devices  34 us (10%)
  matrix products  29.3 us (9%)
  local copies, waits for them, and re-layouts  19.9 us (6%)
  between operations  14.1 us (4%)
  other arithmetic  11 us (3%)
  blocking collectives  10.8 us (3%)
    ppermute x4, waiting for transfers between devices, partner(): return lax.ppermute(value, axis, pairs)  95.4 us
    reduce_scatter x1, waiting for transfers between devices, body(): lax.psum_scatter(jnp.dot(attended, full_out, preferred_element_type=jnp.f...  89.2 us
    all_to_all x1, waiting for transfers between devices, body(): lax.all_to_all(found, 'pool', split_axis=0, concat_axis=0, tiled=True)  14.5 us
    ppermute x4, starting transfers between devices, partner(): return lax.ppermute(value, axis, pairs)  14.2 us
    all_to_all x1, blocking collectives, body(): lax.all_to_all(outgoing, 'pool', split_axis=0, concat_axis=0, tiled=True)  10.8 us
    dot_general x2, local copies, waits for them, and re-layouts, body(): jnp.dot(row_piece, full_query, preferred_element_type=jnp.float32)  8.57 us
    all_to_all x1, starting transfers between devices, body(): lax.all_to_all(wanted, 'pool', split_axis=0, concat_axis=0, tiled=True)  8.47 us
    all_to_all x1, starting transfers between devices, body(): lax.all_to_all(jnp.stack([normed] * lax.axis_size('tp')), 'tp', 0, 0)  7.81 us
  transfers between devices with their start and end apart: 10, of which 7 were waited for; matrix products, arithmetic and copies ran while one was open for 14% of the time, Pallas kernels for 0%

profile of v1, /device:TPU:2, one launch (start us, length us, event | category | flops | bytes accessed | tf_op | source)
XLA Modules:
  0.0 332.5 jit_solution(10483996847982490141)
XLA Ops:
  7.2 1.2 reshape.409
  8.4 2.0 pad_maximum_fusion
  10.5 0.8 reshape.402
  11.2 0.2 convert_reduce_fusion.2
  11.5 0.7 all_to_all.15
  12.2 8.5 %all-to-all-start = ((s32[8,1,6]{2,1,0:T(1,128)}), s32[8,1,6]{2,1,0:T(1,128)S(1)}, u32[]{:S(2)}, u32[]{:S(2)}) async-start(s32[8,1,6]{2,1,0:T(1,128)} %bitcast), calls=%async_computation | async-start | bytes 8192 | tf_op jit(solution)/shard_map/all_to_all | solution.py:124
  20.7 1.1 fusion.16
  21.8 6.5 %all-to-all-done = s32[8,1,6]{2,1,0:T(1,128)S(1)} async-done(((s32[8,1,6]{2,1,0:T(1,128)}), s32[8,1,6]{2,1,0:T(1,128)S(1)}, u32[]{:S(2)}, u32[]{:S(2)}) %all-to-all-start) | async-done | bytes 224 | tf_op jit(solution)/shard_map/all_to_all | solution.py:124
  28.3 0.5 broadcast.351
  28.8 0.7 reduce.3
  29.6 0.7 gather_fusion
  30.4 0.8 broadcast_select_fusion
  31.2 3.4 %all-to-all-start.1 = ((bf16[8,6,2048]{2,1,0:T(8,128)(2,1)}), bf16[8,6,2048]{2,1,0:T(8,128)(2,1)S(1)}, u32[]{:S(2)}, u32[]{:S(2)}) async-start(bf16[8,6,2048]{2,1,0:T(8,128)(2,1)} %broadcast_select_fusion), calls=%async_computation.1 | async-start | bytes 524288 | tf_op jit(solution)/shard_map/all_to_all | solution.py:127
  34.7 14.5 %all-to-all-done.1 = bf16[8,6,2048]{2,1,0:T(8,128)(2,1)S(1)} async-done(((bf16[8,6,2048]{2,1,0:T(8,128)(2,1)}), bf16[8,6,2048]{2,1,0:T(8,128)(2,1)S(1)}, u32[]{:S(2)}, u32[]{:S(2)}) %all-to-all-start.1) | async-done | bytes 196640 | tf_op jit(solution)/shard_map/all_to_all | solution.py:127
  49.2 4.2 %stack.2 = bf16[32,16,8192]{2,1,0:T(8,128)(2,1)} broadcast(bf16[16,8192]{1,0:T(8,128)(2,1)S(1)} %fusion.17), dimensions={1,2} | broadcast | bytes 8650752 | tf_op jit(solution)/shard_map/stack | solution.py:98
  53.5 7.8 %all-to-all-start.2 = ((bf16[32,16,8192]{2,1,0:T(8,128)(2,1)}), bf16[32,16,8192]{2,1,0:T(8,128)(2,1)}, u32[]{:S(2)}, u32[]{:S(2)}) async-start(bf16[32,16,8192]{2,1,0:T(8,128)(2,1)} %stack.2), calls=%async_computation.2 | async-start | bytes 16777216 | tf_op jit(solution)/shard_map/all_to_all | solution.py:98
  61.3 0.7 all-gather.5.cloned.1.call-update
  62.1 0.2 reduce-window.4
  62.5 0.8 fusion.6
  63.4 0.2 convolution_convert_fusion.2
  63.6 0.2 broadcast_in_dim_reshape.3
  64.0 0.2 collective-permute-start
  64.2 1.1 collective-permute-done
  65.3 1.6 collective-permute-start.1
  66.9 0.5 multiply_cosine_fusion.1
  67.4 91.3 %collective-permute-done.1 = bf16[2,512,64]{1,2,0:T(8,128)(2,1)S(1)} collective-permute-done((bf16[2,512,64]{1,2,0:T(8,128)(2,1)S(1)}, bf16[2,512,64]{1,2,0:T(8,128)(2,1)S(1)}, u32[]{:S(2)}, u32[]{:S(2)}) %collective-permute-start.1) | collective-permute-done | bytes 131104 | tf_op jit(solution)/shard_map/ppermute | solution.py:30
  158.8 7.1 %all-to-all-done.2 = bf16[32,16,8192]{2,1,0:T(8,128)(2,1)} async-done(((bf16[32,16,8192]{2,1,0:T(8,128)(2,1)}), bf16[32,16,8192]{2,1,0:T(8,128)(2,1)}, u32[]{:S(2)}, u32[]{:S(2)}) %all-to-all-start.2) | async-done | bytes 8388640 | tf_op jit(solution)/shard_map/all_to_all | solution.py:98
  165.9 6.8 %fusion.13 = bf16[1,512,64]{1,2,0:T(8,128)(2,1)S(1)} fusion(bf16[512,8192]{1,0:T(8,128)(2,1)} %bitcast.6, bf16[8192,320]{1,0:T(8,128)(2,1)} %all-gather.3.cloned.1.call-done), kind=kOutput, calls=%fused_computation.20 | convolution fusion | flops 536903680 | bytes 10551296 | tf_op jit(solution)/shard_map/dot_general | solution.py:103
  172.8 2.2 slice_bitcast_fusion
  175.0 6.3 %copy.49 = bf16[256,8192]{1,0:T(8,128)(2,1)} copy(bf16[256,8192]{0,1:T(8,128)(2,1)} %slice_bitcast_fusion) | data formatting | bytes 8388608 | tf_op jit(solution)/shard_map/dot_general | solution.py:102
  181.4 6.9 %fusion.54 = f32[512,2,128]{0,2,1:T(8,128)S(1)} fusion(bf16[512,8192,1]{1,0,2:T(8,128)(2,1)} %bitcast.22, bf16[2,128,8192]{2,1,0:T(8,128)(2,1)} %bitcast.71), kind=kOutput, calls=%fused_computation.108 | convolution fusion | flops 2147483648 | bytes 13107200 | tf_op jit(solution)/shard_map/dot_general | solution.py:102
  188.4 12.4 %collective-permute-start.3 = (bf16[2,512,64]{1,2,0:T(8,128)(2,1)S(1)}, bf16[2,512,64]{1,2,0:T(8,128)(2,1)S(1)}, u32[]{:S(2)}, u32[]{:S(2)}) collective-permute-start(bf16[2,512,64]{1,2,0:T(8,128)(2,1)S(1)} %maximum_select_fusion.3), channel_id=1, source_target_pairs={{0,2},{1,3},{2,0},{3,1},{4,6},{5,7},{6,4},{7,5},{8,10},{9,11},{10,... | collective-permute-start | bytes 393224 | tf_op jit(solution)/shard_map/ppermute | solution.py:30
  200.7 0.8 subtract_convert_fusion
  201.5 2.9 collective-permute-done.3
  204.5 0.7 fusion.51
  205.2 0.1 copy.57
  205.4 1.2 fusion.32
  206.6 4.6 %fusion.53 = (f32[2,512]{1,0:T(2,128)S(1)}, f32[2,512,1024]{1,2,0:T(8,128)}) fusion(pred[512,1024]{0,1:T(8,128)(4,1)S(1)} %fusion.6, bf16[512,2,64]{0,2,1:T(8,128)(2,1)} %get-tuple-element.21, bf16[512,2,64]{0,2,1:T(8,128)(2,1)} %get-tuple-element.20, bf16[512,64]{1,0:T(8,128)(2,1)S(1)} %get-tuple-element.23, bf16[512,64]{1,0:T(8,128)(2,1)S(1)} %get-tuple-element.22, ...), kind=kOutput, calls=%fused_computation.107 | convolution fusion | flops 273941504 | bytes 5246976 | tf_op jit(solution)/shard_map/while/body/eval_jaxpr/sub | solution.py:181
  211.2 2.7 fusion.9
  214.0 7.8 %convolution_convert_fusion = bf16[512,8192]{1,0:T(8,128)(2,1)} fusion(bf16[512,256]{0,1:T(8,128)(2,1)S(1)} %bitcast.74, bf16[256,8192]{1,0:T(8,128)(2,1)} %all-gather.5.cloned.1.call-done), kind=kOutput, calls=%fused_computation.2 | convolution fusion | flops 2151677952 | bytes 12845056 | tf_op jit(solution)/shard_map/dot_general | solution.py:193
  221.8 0.6 copy-done.5
  222.4 0.2 convert_reduce_fusion
  223.0 0.2 reshape.416
  223.2 0.3 convolution_convert_fusion.1
  223.6 10.8 %all_to_all.24 = bf16[8,2,2048]{2,1,0:T(2,128)(2,1)S(1)} all-to-all(bf16[8,2,2048]{2,1,0:T(2,128)(2,1)S(1)} %reshape.417), channel_id=1, replica_groups=mesh['pool'=8,'tp'=32] {'pool'}, dimensions={0} | all-to-all | bytes 131072 | tf_op jit(solution)/shard_map/all_to_all | solution.py:160
  234.3 0.7 reshape.418
  235.0 89.2 %reduce-scatter.2.cloned.1.call-done = bf16[16,8192]{1,0:T(8,128)(2,1)} async-done(((bf16[512,8192]{1,0:T(8,128)(2,1)}), bf16[16,8192]{1,0:T(8,128)(2,1)}) %reduce-scatter.2.cloned.1.call-update) | async-done | bytes 262160 | tf_op jit(solution)/shard_map/reduce_scatter | solution.py:192
  324.2 1.8 convert_add_fusion
  (51 shorter events, 1.8 us)
Async XLA Ops:
  7.2 22.4 %copy-start = (bf16[512,1,2048]{2,0,1:T(8,128)(2,1)S(1)}, bf16[512,1,2048]{2,0,1:T(8,128)(2,1)}, u32[]{:S(2)}) copy-start(bf16[512,1,2048]{2,0,1:T(8,128)(2,1)} %param.15) | copy-start | bytes 6291460
  7.2 27.4 %copy-start.2 = (bf16[16,8192]{1,0:T(8,128)(2,1)S(1)}, bf16[16,8192]{1,0:T(8,128)(2,1)}, u32[]{:S(2)}) copy-start(bf16[16,8192]{1,0:T(8,128)(2,1)} %param.8) | copy-start | bytes 786436
  7.2 158.7 %all-gather.3.cloned.1.call-start = ((), (), s32[]{:S(2)}) async-start(), calls=%async_computation.5 | async-start | bytes 7077888 | tf_op jit(solution)/shard_map/all_gather | solution.py:24
  12.2 16.1 %all-to-all-start = ((s32[8,1,6]{2,1,0:T(1,128)}), s32[8,1,6]{2,1,0:T(1,128)S(1)}, u32[]{:S(2)}, u32[]{:S(2)}) async-start(s32[8,1,6]{2,1,0:T(1,128)} %bitcast), calls=%async_computation | async-start | bytes 8192 | tf_op jit(solution)/shard_map/all_to_all | solution.py:124
  31.2 18.1 %all-to-all-start.1 = ((bf16[8,6,2048]{2,1,0:T(8,128)(2,1)}), bf16[8,6,2048]{2,1,0:T(8,128)(2,1)S(1)}, u32[]{:S(2)}, u32[]{:S(2)}) async-start(bf16[8,6,2048]{2,1,0:T(8,128)(2,1)} %broadcast_select_fusion), calls=%async_computation.1 | async-start | bytes 524288 | tf_op jit(solution)/shard_map/all_to_all | solution.py:127
  53.5 8.6 %copy-start.4 = (s32[1,4]{1,0:T(1,128)S(1)}, s32[1,4]{1,0:T(1,128)}, u32[]{:S(2)}) copy-start(s32[1,4]{1,0:T(1,128)} %param.9) | copy-start | bytes 52
  53.5 9.0 %copy-start.3 = (s32[1024]{0:T(1024)S(1)}, s32[1024]{0:T(1024)}, u32[]{:S(2)}) copy-start(s32[1024]{0:T(1024)} %constant.140.clone.1) | copy-start | bytes 12292
  53.5 112.4 %all-to-all-start.2 = ((bf16[32,16,8192]{2,1,0:T(8,128)(2,1)}), bf16[32,16,8192]{2,1,0:T(8,128)(2,1)}, u32[]{:S(2)}, u32[]{:S(2)}) async-start(bf16[32,16,8192]{2,1,0:T(8,128)(2,1)} %stack.2), calls=%async_computation.2 | async-start | bytes 16777216 | tf_op jit(solution)/shard_map/all_to_all | solution.py:98
  61.3 152.7 %all-gather.5.cloned.1.call-start = ((), (), s32[]{:S(2)}) async-start(), calls=%async_computation.6 | async-start | bytes 4718592 | tf_op jit(solution)/shard_map/all_gather | solution.py:191
  62.0 262.1 %reduce-scatter.2.cloned.1.call-start = ((), (), s32[]{:S(2)}) async-start(), calls=%async_computation.7 | async-start | bytes 8650752 | tf_op jit(solution)/shard_map/reduce_scatter | solution.py:192
  64.0 1.3 collective-permute-start
  65.3 93.4 %collective-permute-start.1 = (bf16[2,512,64]{1,2,0:T(8,128)(2,1)S(1)}, bf16[2,512,64]{1,2,0:T(8,128)(2,1)S(1)}, u32[]{:S(2)}, u32[]{:S(2)}) collective-permute-start(bf16[2,512,64]{1,2,0:T(8,128)(2,1)S(1)} %maximum_select_fusion.2), channel_id=1, source_target_pairs={{0,2},{1,3},{2,0},{3,1},{4,6},{5,7},{6,4},{7,5},{8,10},{9,11},{10,... | collective-permute-start | bytes 393224 | tf_op jit(solution)/shard_map/ppermute | solution.py:30
  165.9 6.9 %copy-start.1 = (bf16[8192,320]{1,0:T(8,128)(2,1)S(1)}, bf16[8192,320]{1,0:T(8,128)(2,1)}, u32[]{:S(2)}) copy-start(bf16[8192,320]{1,0:T(8,128)(2,1)} %all-gather.3.cloned.1.call-done) | copy-start | bytes 15728644
  172.7 15.6 %collective-permute-start.2 = (bf16[1,512,64]{1,2,0:T(8,128)(2,1)S(1)}, bf16[1,512,64]{1,2,0:T(8,128)(2,1)S(1)}, u32[]{:S(2)}, u32[]{:S(2)}) collective-permute-start(bf16[1,512,64]{1,2,0:T(8,128)(2,1)S(1)} %fusion.13), channel_id=1, source_target_pairs={{0,1},{1,0},{2,3},{3,2},{4,5},{5,4},{6,7},{7,6},{8,9},{9,8},{10,11... | collective-permute-start | bytes 196616 | tf_op jit(solution)/shard_map/ppermute | solution.py:30
  188.4 16.1 %collective-permute-start.3 = (bf16[2,512,64]{1,2,0:T(8,128)(2,1)S(1)}, bf16[2,512,64]{1,2,0:T(8,128)(2,1)S(1)}, u32[]{:S(2)}, u32[]{:S(2)}) collective-permute-start(bf16[2,512,64]{1,2,0:T(8,128)(2,1)S(1)} %maximum_select_fusion.3), channel_id=1, source_target_pairs={{0,2},{1,3},{2,0},{3,1},{4,6},{5,7},{6,4},{7,5},{8,10},{9,11},{10,... | collective-permute-start | bytes 393224 | tf_op jit(solution)/shard_map/ppermute | solution.py:30
  221.7 0.7 copy-start.5
Sparse Core Ops, SparseCore 0:
  10.6 82.9 all-gather.2
  95.4 53.3 all-gather.4
  221.9 102.2 reduce-scatter.1
